TPU v7x, 32 devices: a whole 2x2x4 slice. The times are simulated.
32 devices in a mesh: dp: 8 (over y, x, core), ctx: 4 (over z).
Axes of the slice: x: 2, y: 2, z: 4, core: 2. Of those that a mesh axis runs over, the one named last changes fastest.
Arguments:
- tokens: bfloat16 [16, 2048, 1088], P('dp', 'ctx'), may hold values from -6 to 6
- segments: int32 [16, 2048], P('dp'), may hold values from 0 to 31, never falling along the last dimension, each value on 1 to 1024 neighbouring positions
- adapter_index: int32 [16], P('dp'), may hold values from 0 to 7
- w_qkv: bfloat16 [1088, 3264], P('ctx', 'dp'), may hold values from -0.1875 to 0.1875
- w_out: bfloat16 [1088, 1088], P('ctx', 'dp'), may hold values from -0.75 to 0.75
- w_fc1: bfloat16 [1088, 4352], P('ctx', 'dp'), may hold values from -0.1875 to 0.1875
- w_fc2: bfloat16 [4352, 1088], P('ctx', 'dp'), may hold values from -0.09375 to 0.09375
- gain_one: float32 [1088], replicated, may hold values from 0.1 to 1.9
- gain_two: float32 [1088], replicated, may hold values from 0.1 to 1.9
- qkv_down: bfloat16 [128, 1088], replicated, may hold values from -0.1875 to 0.1875
- qkv_up: bfloat16 [128, 3264], replicated, may hold values from -0.75 to 0.75
- out_down: bfloat16 [128, 1088], replicated, may hold values from -0.1875 to 0.1875
- out_up: bfloat16 [128, 1088], replicated, may hold values from -0.75 to 0.75
- fc1_down: bfloat16 [128, 1088], replicated, may hold values from -0.1875 to 0.1875
- fc1_up: bfloat16 [128, 4352], replicated, may hold values from -0.75 to 0.75
- fc2_down: bfloat16 [128, 4352], replicated, may hold values from -0.09375 to 0.09375
- fc2_up: bfloat16 [128, 1088], replicated, may hold values from -0.75 to 0.75
- cotangent: bfloat16 [16, 2048, 1088], P('dp', 'ctx'), may hold values from -6 to 6
Outputs:
- output: bfloat16 [16, 2048, 1088], P('dp', 'ctx')
- input_grad: bfloat16 [16, 2048, 1088], P('dp', 'ctx')
- qkv_down_grad: float32 [128, 1088], P('dp', 'ctx')
- qkv_up_grad: float32 [128, 3264], P('dp', 'ctx')
- out_down_grad: float32 [128, 1088], P('dp', 'ctx')
- out_up_grad: float32 [128, 1088], P('dp', 'ctx')
- fc1_down_grad: float32 [128, 1088], P('dp', 'ctx')
- fc1_up_grad: float32 [128, 4352], P('dp', 'ctx')
- fc2_down_grad: float32 [128, 4352], P('dp', 'ctx')
- fc2_up_grad: float32 [128, 1088], P('dp', 'ctx')
Inputs may be any that keep to these rules, and one draw needn't show every extreme that they name: `segments`: document numbers never fall along a sequence; a document holds at most 1024 tokens.
All inputs are finite; a program needn't handle non-finite values.
Results may differ from a plain program's by a relative error of at most 0.023.
Values may be sent and summed in bfloat16 or wider, within the bound.
No kernel may reach another device: no remote copies, remote signals or barrier semaphores. Data moves between devices by JAX's collectives and lax.ppermute only.
A program may use at most 320 MiB of HBM per device.

v0:
```python
import jax
import jax.numpy as jnp
from jax import lax
from jax.sharding import PartitionSpec as P

HEADS = 17
ADAPTERS = 8
eps = 1e-05
neg_big = -1e30


def norm_rows(vector, gain):
    center = vector - jnp.mean(vector, -1, keepdims=True)
    inv_std = lax.rsqrt(jnp.mean(center * center, -1, keepdims=True) + eps)
    scaled = center * inv_std
    return (scaled * gain, scaled, inv_std)


def norm_back(grad, scaled, inv_std, gain):
    inner = grad * gain
    return inv_std * (
        inner
        - jnp.mean(inner, -1, keepdims=True)
        - scaled * jnp.mean(inner * scaled, -1, keepdims=True)
    )


def select_adapter(picker, stack):
    shaped = stack.reshape(picker.shape[1], stack.shape[0] // picker.shape[1], stack.shape[1])
    return jnp.einsum("sa,arw->srw", picker, shaped, preferred_element_type=jnp.float32).astype(
        jnp.bfloat16
    )


def project(inputs, weight, down_rows, up_rows):
    main_part = jnp.einsum("slw,wv->slv", inputs, weight, preferred_element_type=jnp.float32)
    lowered = jnp.einsum(
        "slw,srw->slr", inputs, down_rows, preferred_element_type=jnp.float32
    ).astype(jnp.bfloat16)
    return (
        main_part
        + jnp.einsum("slr,srv->slv", lowered, up_rows, preferred_element_type=jnp.float32),
        lowered,
    )


def project_back(grad_low, inputs, lowered, weight, down_rows, up_rows):
    grad_in = jnp.einsum("slv,wv->slw", grad_low, weight, preferred_element_type=jnp.float32)
    grad_mid = jnp.einsum(
        "slv,srv->slr", grad_low, up_rows, preferred_element_type=jnp.float32
    ).astype(jnp.bfloat16)
    grad_in = grad_in + jnp.einsum(
        "slr,srw->slw", grad_mid, down_rows, preferred_element_type=jnp.float32
    )
    grad_up = jnp.einsum("slr,slv->srv", lowered, grad_low, preferred_element_type=jnp.float32)
    grad_down = jnp.einsum("slr,slw->srw", grad_mid, inputs, preferred_element_type=jnp.float32)
    return (grad_in, grad_down, grad_up)


def gather_weights(part_qkv, part_out, part_fc1, part_fc2):
    wide_qkv, wide_out, wide_fc1, wide_fc2 = (
        lax.all_gather(part_qkv, "dp", axis=1, tiled=True),
        lax.all_gather(part_out, "dp", axis=1, tiled=True),
        lax.all_gather(part_fc1, "dp", axis=1, tiled=True),
        lax.all_gather(part_fc2, "dp", axis=1, tiled=True),
    )
    return (
        lax.all_gather(wide_qkv, "ctx", axis=0, tiled=True),
        lax.all_gather(wide_out, "ctx", axis=0, tiled=True),
        lax.all_gather(wide_fc1, "ctx", axis=0, tiled=True),
        lax.all_gather(wide_fc2, "ctx", axis=0, tiled=True),
    )


def block_mask(query_pos, query_seg, key_pos, key_seg):
    causal = key_pos[None, None, :] <= query_pos[None, :, None]
    same_doc = key_seg[:, None, :] == query_seg[:, :, None]
    return (causal & same_doc)[:, None]


def per_device(
    tokens,
    segments,
    adapter_index,
    w_qkv,
    w_out,
    w_fc1,
    w_fc2,
    gain_one,
    gain_two,
    qkv_down,
    qkv_up,
    out_down,
    out_up,
    fc1_down,
    fc1_up,
    fc2_down,
    fc2_up,
    cotangent,
):
    seq_count, row_count, width = tokens.shape
    head_dim = width // HEADS
    scale = head_dim ** (-0.5)
    full_qkv, full_out, full_fc1, full_fc2 = gather_weights(w_qkv, w_out, w_fc1, w_fc2)
    picker = (adapter_index[:, None] == jnp.arange(ADAPTERS, dtype=jnp.int32)[None, :]).astype(
        jnp.bfloat16
    )
    stacks = (qkv_down, qkv_up, out_down, out_up, fc1_down, fc1_up, fc2_down, fc2_up)
    chosen = [select_adapter(picker, stack) for stack in stacks]
    first_query = lax.axis_index("ctx") * row_count
    query_pos = first_query + jnp.arange(row_count, dtype=jnp.int32)
    query_seg = lax.dynamic_slice_in_dim(segments, first_query, row_count, 1)
    stream = tokens.astype(jnp.float32)
    normed_one, scaled_one, inv_one = norm_rows(stream, gain_one)
    normed_one = normed_one.astype(jnp.bfloat16)
    merged, lowered_qkv = project(normed_one, full_qkv, chosen[0], chosen[1])
    merged = merged.astype(jnp.bfloat16)
    queries = merged[..., :width].reshape(seq_count, row_count, HEADS, head_dim)
    key_vals = merged[..., width:]

    def attend(state, keys, values, mask):
        peak_old, total, accum = state
        scores = (
            jnp.einsum("sqhd,skhd->shqk", queries, keys, preferred_element_type=jnp.float32) * scale
        )
        scores = jnp.where(mask, scores, neg_big)
        peak_new = jnp.maximum(peak_old, jnp.max(scores, -1))
        expo_term = jnp.where(mask, jnp.exp(scores - peak_new[..., None]), 0.0)
        fade = jnp.exp(peak_old - peak_new)
        total = total * fade + jnp.sum(expo_term, -1)
        accum = accum * jnp.swapaxes(fade, 1, 2)[..., None] + jnp.einsum(
            "shqk,skhd->sqhd",
            expo_term.astype(jnp.bfloat16),
            values,
            preferred_element_type=jnp.float32,
        )
        return (peak_new, total, accum)

    start_state = (
        jnp.full((seq_count, HEADS, row_count), neg_big, jnp.float32),
        jnp.zeros((seq_count, HEADS, row_count), jnp.float32),
        jnp.zeros((seq_count, row_count, HEADS, head_dim), jnp.float32),
    )
    piece = lax.all_gather(key_vals, "ctx", axis=1, tiled=True)
    key_count = piece.shape[1]
    block = 512

    def key_step(turn, inner):
        offset = turn * block
        part = lax.dynamic_slice_in_dim(piece, turn * block, block, 1)
        key_pos = offset + jnp.arange(block, dtype=jnp.int32)
        key_seg = lax.dynamic_slice_in_dim(segments, offset, block, 1)
        mask = block_mask(query_pos, query_seg, key_pos, key_seg)
        keys = part[..., :width].reshape(seq_count, block, HEADS, head_dim)
        values = part[..., width:].reshape(seq_count, block, HEADS, head_dim)
        return attend(inner, keys, values, mask)

    peak_end, total_end, accum_end = lax.fori_loop(0, key_count // block, key_step, start_state)
    attended = (accum_end / jnp.swapaxes(total_end, 1, 2)[..., None]).reshape(
        seq_count, row_count, width
    )
    log_total = peak_end + jnp.log(total_end)
    attended_low = attended.astype(jnp.bfloat16)
    branch, lowered_out = project(attended_low, full_out, chosen[2], chosen[3])
    middle = stream + branch
    normed_two, scaled_two, inv_two = norm_rows(middle, gain_two)
    normed_two = normed_two.astype(jnp.bfloat16)
    hidden, lowered_fc1 = project(normed_two, full_fc1, chosen[4], chosen[5])
    active = jax.nn.gelu(hidden, approximate=True).astype(jnp.bfloat16)
    mlp_out, lowered_fc2 = project(active, full_fc2, chosen[6], chosen[7])
    output = (middle + mlp_out).astype(jnp.bfloat16)
    full_qkv, full_out, full_fc1, full_fc2 = gather_weights(w_qkv, w_out, w_fc1, w_fc2)
    grad_active, grad_fc2_down, grad_fc2_up = project_back(
        cotangent, active, lowered_fc2, full_fc2, chosen[6], chosen[7]
    )
    gelu_value, gelu_pull = jax.vjp(
        lambda inner_in: jax.nn.gelu(inner_in, approximate=True), hidden
    )
    grad_hidden = gelu_pull(grad_active)[0].astype(jnp.bfloat16)
    grad_two, grad_fc1_down, grad_fc1_up = project_back(
        grad_hidden, normed_two, lowered_fc1, full_fc1, chosen[4], chosen[5]
    )
    grad_middle = cotangent.astype(jnp.float32) + norm_back(grad_two, scaled_two, inv_two, gain_two)
    grad_branch = grad_middle.astype(jnp.bfloat16)
    grad_att, grad_out_down, grad_out_up = project_back(
        grad_branch, attended_low, lowered_out, full_out, chosen[2], chosen[3]
    )
    grad_att = grad_att.astype(jnp.bfloat16)
    grad_att_heads = grad_att.reshape(seq_count, row_count, HEADS, head_dim)
    delta = jnp.swapaxes(
        jnp.sum(
            (grad_att.astype(jnp.float32) * attended).reshape(
                seq_count, row_count, HEADS, head_dim
            ),
            -1,
        ),
        1,
        2,
    )
    all_keys = lax.all_gather(key_vals, "ctx", axis=1, tiled=True)
    key_total = all_keys.shape[1]
    back_block = 512

    def back_step(turn, state):
        offset = turn * back_block
        part = lax.dynamic_slice_in_dim(all_keys, offset, back_block, 1)
        key_pos = offset + jnp.arange(back_block, dtype=jnp.int32)
        key_seg = lax.dynamic_slice_in_dim(segments, offset, back_block, 1)
        mask = block_mask(query_pos, query_seg, key_pos, key_seg)
        keys = part[..., :width].reshape(seq_count, back_block, HEADS, head_dim)
        values = part[..., width:].reshape(seq_count, back_block, HEADS, head_dim)
        grad_query, grad_keys = state
        scores = (
            jnp.einsum("sqhd,skhd->shqk", queries, keys, preferred_element_type=jnp.float32) * scale
        )
        probs = jnp.where(mask, jnp.exp(scores - log_total[..., None]), 0.0)
        grad_probs = jnp.einsum(
            "sqhd,skhd->shqk", grad_att_heads, values, preferred_element_type=jnp.float32
        )
        grad_scores = (probs * (grad_probs - delta[..., None])).astype(jnp.bfloat16)
        grad_query = grad_query + jnp.einsum(
            "shqk,skhd->sqhd", grad_scores, keys, preferred_element_type=jnp.float32
        )
        grad_k = (
            jnp.einsum("shqk,sqhd->skhd", grad_scores, queries, preferred_element_type=jnp.float32)
            * scale
        )
        grad_v = jnp.einsum(
            "shqk,sqhd->skhd",
            probs.astype(jnp.bfloat16),
            grad_att_heads,
            preferred_element_type=jnp.float32,
        )
        joined = jnp.concatenate(
            [
                grad_k.reshape(seq_count, back_block, width),
                grad_v.reshape(seq_count, back_block, width),
            ],
            -1,
        )
        return (grad_query, lax.dynamic_update_slice_in_dim(grad_keys, joined, offset, 1))

    back_start = (
        jnp.zeros((seq_count, row_count, HEADS, head_dim), jnp.float32),
        jnp.zeros((seq_count, key_total, 2 * width), jnp.float32),
    )
    grad_query, grad_keys = lax.fori_loop(0, key_total // back_block, back_step, back_start)
    own_key_grads = lax.psum_scatter(
        grad_keys.astype(jnp.bfloat16), "ctx", scatter_dimension=1, tiled=True
    ).astype(jnp.float32)
    grad_merged = jnp.concatenate(
        [(grad_query * scale).reshape(seq_count, row_count, width), own_key_grads], -1
    ).astype(jnp.bfloat16)
    grad_one, grad_qkv_down, grad_qkv_up = project_back(
        grad_merged, normed_one, lowered_qkv, full_qkv, chosen[0], chosen[1]
    )
    input_grad = (grad_middle + norm_back(grad_one, scaled_one, inv_one, gain_one)).astype(
        jnp.bfloat16
    )
    picker_wide = picker.astype(jnp.float32)

    def spread(grad):
        return jnp.einsum("sa,srw->arw", picker_wide, grad).reshape(
            ADAPTERS * grad.shape[1], grad.shape[2]
        )

    term_a, term_b, term_c, term_d, term_e, term_f, term_g, term_h = [
        spread(grad)
        for grad in (
            grad_qkv_down,
            grad_qkv_up,
            grad_out_down,
            grad_out_up,
            grad_fc1_down,
            grad_fc1_up,
            grad_fc2_down,
            grad_fc2_up,
        )
    ]
    part_a, part_b, part_c, part_d, part_e, part_f, part_g, part_h = (
        lax.psum_scatter(
            term_a.astype(jnp.bfloat16), "ctx", scatter_dimension=1, tiled=True
        ).astype(jnp.float32),
        lax.psum_scatter(
            term_b.astype(jnp.bfloat16), "ctx", scatter_dimension=1, tiled=True
        ).astype(jnp.float32),
        lax.psum_scatter(
            term_c.astype(jnp.bfloat16), "ctx", scatter_dimension=1, tiled=True
        ).astype(jnp.float32),
        lax.psum_scatter(
            term_d.astype(jnp.bfloat16), "ctx", scatter_dimension=1, tiled=True
        ).astype(jnp.float32),
        lax.psum_scatter(
            term_e.astype(jnp.bfloat16), "ctx", scatter_dimension=1, tiled=True
        ).astype(jnp.float32),
        lax.psum_scatter(
            term_f.astype(jnp.bfloat16), "ctx", scatter_dimension=1, tiled=True
        ).astype(jnp.float32),
        lax.psum_scatter(
            term_g.astype(jnp.bfloat16), "ctx", scatter_dimension=1, tiled=True
        ).astype(jnp.float32),
        lax.psum_scatter(
            term_h.astype(jnp.bfloat16), "ctx", scatter_dimension=1, tiled=True
        ).astype(jnp.float32),
    )
    final_a, final_b, final_c, final_d, final_e, final_f, final_g, final_h = (
        lax.psum_scatter(part_a.astype(jnp.bfloat16), "dp", scatter_dimension=0, tiled=True).astype(
            jnp.float32
        ),
        lax.psum_scatter(part_b.astype(jnp.bfloat16), "dp", scatter_dimension=0, tiled=True).astype(
            jnp.float32
        ),
        lax.psum_scatter(part_c.astype(jnp.bfloat16), "dp", scatter_dimension=0, tiled=True).astype(
            jnp.float32
        ),
        lax.psum_scatter(part_d.astype(jnp.bfloat16), "dp", scatter_dimension=0, tiled=True).astype(
            jnp.float32
        ),
        lax.psum_scatter(part_e.astype(jnp.bfloat16), "dp", scatter_dimension=0, tiled=True).astype(
            jnp.float32
        ),
        lax.psum_scatter(part_f.astype(jnp.bfloat16), "dp", scatter_dimension=0, tiled=True).astype(
            jnp.float32
        ),
        lax.psum_scatter(part_g.astype(jnp.bfloat16), "dp", scatter_dimension=0, tiled=True).astype(
            jnp.float32
        ),
        lax.psum_scatter(part_h.astype(jnp.bfloat16), "dp", scatter_dimension=0, tiled=True).astype(
            jnp.float32
        ),
    )
    return (
        output,
        input_grad,
        final_a,
        final_b,
        final_c,
        final_d,
        final_e,
        final_f,
        final_g,
        final_h,
    )


def solution(mesh):
    return jax.shard_map(
        per_device,
        mesh=mesh,
        in_specs=(
            P("dp", "ctx", None),
            P("dp", None),
            P("dp"),
            P("ctx", "dp"),
            P("ctx", "dp"),
            P("ctx", "dp"),
            P("ctx", "dp"),
            P(),
            P(),
            P(),
            P(),
            P(),
            P(),
            P(),
            P(),
            P(),
            P(),
            P("dp", "ctx", None),
        ),
        out_specs=(
            P("dp", "ctx", None),
            P("dp", "ctx", None),
            P("dp", "ctx"),
            P("dp", "ctx"),
            P("dp", "ctx"),
            P("dp", "ctx"),
            P("dp", "ctx"),
            P("dp", "ctx"),
            P("dp", "ctx"),
            P("dp", "ctx"),
        ),
        check_vma=False,
    )
```

profile of v0, /device:TPU:0, one launch (start us, length us, event | category | flops | bytes accessed | tf_op | source)
XLA Modules:
  0.0 1883.6 jit_solution(2579130718959137755)
XLA Ops:
  8.0 33.1 %all-gather.23.cloned.1.call-done = bf16[8,408,272]{1,2,0:T(8,128)(2,1)} async-done(((bf16[1,408,272]{1,2,0:T(8,128)(2,1)}), bf16[8,408,272]{1,2,0:T(8,128)(2,1)}) %all-gather.23.cloned.1.call-update) | async-done | bytes 1775632 | tf_op jit(solution)/shard_map/all_gather | solution.py:62
  45.3 5.2 reshape.262
  65.5 116.1 %all-gather.11.cloned.1.call-done = bf16[1088,3264]{1,0:T(8,128)(2,1)} async-done(((bf16[272,3264]{1,0:T(8,128)(2,1)}), bf16[1088,3264]{1,0:T(8,128)(2,1)}) %all-gather.11.cloned.1.call-update) | async-done | bytes 7102480 | tf_op jit(solution)/shard_map/all_gather | solution.py:68
  181.6 12.5 fusion.39
  202.0 13.2 all_gather.39
  220.9 5.7 reshape.264
  245.3 8.6 fusion.93
  254.0 5.2 copy.185
  259.4 294.8 %all-gather.13.cloned.1.call-done = bf16[2,2048,2176]{1,2,0:T(8,128)(2,1)} async-done(((bf16[2,512,2176]{1,2,0:T(8,128)(2,1)}), bf16[2,2048,2176]{1,2,0:T(8,128)(2,1)}) %all-gather.13.cloned.1.call-update) | async-done | bytes 17825808 | tf_op jit(solution)/shard_map/all_gather | solution.py:144
  554.2 220.1 %while.34 = (s32[]{:T(128)}, f32[2,17,512]{2,1,0:T(8,128)S(1)}, f32[2,17,512]{2,1,0:T(8,128)S(1)}, f32[2,512,17,64]{1,3,2,0:T(8,128)}, s32[2,2048]{1,0:T(2,128)}...) while((s32[]{:T(128)}, f32[2,17,512]{2,1,0:T(8,128)S(1)}, ...), condition=%wide.region_5.6_spmd.clone, body=%wide.region_2.5_spmd.clone.sunk | while | flops 2402327552 | bytes 135225584 | solution.py:158
  559.6 14.4 fusion.239
  574.0 15.4 fusion.241
  589.4 17.9 bitcast_add_fusion.4
  612.8 15.8 fusion.239
  628.6 15.4 fusion.241
  644.1 20.1 %bitcast_add_fusion.4 = f32[2,512,17,64]{1,3,2,0:T(8,128)} fusion(f32[2,512,17,64]{1,3,2,0:T(8,128)} %get-tuple-element.657, f32[2,512,17]{1,2,0:T(8,128)S(1)} %get-tuple-element.623, pred[]{:T(512)S(6)} %compare.6, bf16[2,512,17,64]{1,3,2,0:T(8,128)(2,1)} %bitcast.272, f32[2,17,512,512]{3,2,1,0:T(8,128)} %get-tuple-element.622, ...), kind=kOutput, calls=%fused_computation.9.clone.1 | convolution fusion | flops 1188757504 | bytes 47456256 | tf_op jit(solution)/shard_map/while/body/eval_jaxpr/shqk,skhd->sqhd/dot_general | solution.py:131
  669.7 14.4 fusion.239
  684.1 15.4 fusion.241
  699.5 19.9 %bitcast_add_fusion.4 = f32[2,512,17,64]{1,3,2,0:T(8,128)} fusion(f32[2,512,17,64]{1,3,2,0:T(8,128)} %get-tuple-element.657, f32[2,512,17]{1,2,0:T(8,128)S(1)} %get-tuple-element.623, pred[]{:T(512)S(6)} %compare.6, bf16[2,512,17,64]{1,3,2,0:T(8,128)(2,1)} %bitcast.272, f32[2,17,512,512]{3,2,1,0:T(8,128)} %get-tuple-element.622, ...), kind=kOutput, calls=%fused_computation.9.clone.1 | convolution fusion | flops 1188757504 | bytes 47456256 | tf_op jit(solution)/shard_map/while/body/eval_jaxpr/shqk,skhd->sqhd/dot_general | solution.py:131
  724.9 14.3 fusion.239
  739.2 15.3 fusion.241
  754.5 19.5 %bitcast_add_fusion.4 = f32[2,512,17,64]{1,3,2,0:T(8,128)} fusion(f32[2,512,17,64]{1,3,2,0:T(8,128)} %get-tuple-element.657, f32[2,512,17]{1,2,0:T(8,128)S(1)} %get-tuple-element.623, pred[]{:T(512)S(6)} %compare.6, bf16[2,512,17,64]{1,3,2,0:T(8,128)(2,1)} %bitcast.272, f32[2,17,512,512]{3,2,1,0:T(8,128)} %get-tuple-element.622, ...), kind=kOutput, calls=%fused_computation.9.clone.1 | convolution fusion | flops 1188757504 | bytes 47456256 | tf_op jit(solution)/shard_map/while/body/eval_jaxpr/shqk,skhd->sqhd/dot_general | solution.py:131
  781.6 6.3 fusion.77
  792.9 8.7 fusion.97
  801.5 28.2 %multiply_convert_fusion = (bf16[2,512,4352]{2,1,0:T(8,128)(2,1)}, f32[2,512,4352]{2,1,0:T(8,128)}) fusion(f32[2,512,4352]{2,1,0:T(8,128)} %fusion.97, bf16[2,512,1088]{1,2,0:T(8,128)(2,1)} %copy-done.17, bf16[1088,4352]{1,0:T(8,128)(2,1)} %all-gather.17.cloned.1.call-done), kind=kOutput, calls=%fused_computation.53 | convolution fusion | flops 9741795328 | bytes 56262656 | tf_op jit(solution)/shard_map/slw,wv->slv/dot_general | solution.py:36
  829.7 6.1 convolution_convert_fusion.17
  837.9 113.6 %all-gather.21.cloned.1.call-done = bf16[4352,1088]{1,0:T(8,128)(2,1)} async-done(((bf16[1088,1088]{1,0:T(8,128)(2,1)}), bf16[4352,1088]{1,0:T(8,128)(2,1)}) %all-gather.21.cloned.1.call-update) | async-done | bytes 9469968 | tf_op jit(solution)/shard_map/all_gather | solution.py:71
  951.5 26.8 %fusion.30 = bf16[2,512,4352]{2,1,0:T(8,128)(2,1)} fusion(f32[2,512,4352]{2,1,0:T(8,128)} %get-tuple-element.487, f32[2,512,4352]{2,1,0:T(8,128)} %fusion.93, bf16[2,512,1088]{1,2,0:T(8,128)(2,1)} %param.39, bf16[4352,1088]{1,0:T(8,128)(2,1)} %all-gather.21.cloned.1.call-done), kind=kOutput, calls=%fused_computation.52 | convolution fusion | flops 9790816256 | bytes 56262656 | tf_op jit(solution)/shard_map/slv,wv->slw/dot_general | solution.py:48
  978.3 6.1 convolution_convert_fusion.16
  989.3 17.1 fusion.159
  1042.4 10.1 reduce-scatter.56.cloned.1.call-done
  1054.2 8.1 fusion.75
  1062.4 18.9 %reduce-scatter.64.cloned.1.call-done = bf16[1088,128]{1,0:T(8,128)(2,1)} async-done(((bf16[4352,128]{1,0:T(8,128)(2,1)}), bf16[1088,128]{1,0:T(8,128)(2,1)}) %reduce-scatter.64.cloned.1.call-update) | async-done | bytes 278544
  1083.2 7.2 bitcast_multiply_fusion.1
  1093.3 17.0 reduce-scatter.62.cloned.1.call-done
  1112.3 6.4 broadcast_in_dim.126
  1118.7 338.8 %while.35 = (s32[]{:T(128)}, f32[2,512,17,64]{1,3,2,0:T(8,128)}, bf16[2,2048,2176]{1,2,0:T(8,128)(2,1)}, bf16[2,2048,2176]{1,2,0:T(8,128)(2,1)}, s32[2,2048]{1,0...) while((s32[]{:T(128)}, f32[2,512,17,64]{1,3,2,0:T(8,128)}, ...), condition=%wide.region_12.13_spmd.clone, body=%wide.region_11.12_spmd.clone.sunk | while | flops 5808063488 | bytes 236294480 | solution.py:247
  1125.1 15.6 fusion.253
  1140.7 16.6 fusion.255
  1157.3 22.0 %fusion.254 = bf16[2,17,512,512]{2,3,1,0:T(8,128)(2,1)} fusion(f32[2,17,512,512]{3,2,1,0:T(8,128)} %fusion.253, bf16[2,512,17,64]{1,3,2,0:T(8,128)(2,1)} %bitcast.274, bf16[2,512,17,64]{1,3,2,0:T(8,128)(2,1)} %get-tuple-element.722, f32[2,17,512]{2,1,0:T(8,128)S(1)} %get-tuple-element.723, f32[2,17,512]{2,1,0:T(8,128)S(1)} %get-tuple-element.721, ...), kind=kOutput, calls=%fused_computation.27.clone.1 | convolution fusion | flops 1194328064 | bytes 58597376 | tf_op jit(solution)/shard_map/while/body/eval_jaxpr/sqhd,skhd->shqk/dot_general | solution.py:217
  1179.3 11.0 bitcast_add_fusion.5
  1190.3 10.0 broadcast_multiply_fusion.8
  1208.8 15.6 fusion.253
  1224.4 16.7 fusion.255
  1241.0 22.0 %fusion.254 = bf16[2,17,512,512]{2,3,1,0:T(8,128)(2,1)} fusion(f32[2,17,512,512]{3,2,1,0:T(8,128)} %fusion.253, bf16[2,512,17,64]{1,3,2,0:T(8,128)(2,1)} %bitcast.274, bf16[2,512,17,64]{1,3,2,0:T(8,128)(2,1)} %get-tuple-element.722, f32[2,17,512]{2,1,0:T(8,128)S(1)} %get-tuple-element.723, f32[2,17,512]{2,1,0:T(8,128)S(1)} %get-tuple-element.721, ...), kind=kOutput, calls=%fused_computation.27.clone.1 | convolution fusion | flops 1194328064 | bytes 58597376 | tf_op jit(solution)/shard_map/while/body/eval_jaxpr/sqhd,skhd->shqk/dot_general | solution.py:217
  1263.0 12.3 bitcast_add_fusion.5
  1275.3 9.9 broadcast_multiply_fusion.8
  1293.8 15.6 fusion.253
  1309.4 16.6 fusion.255
  1326.0 22.0 %fusion.254 = bf16[2,17,512,512]{2,3,1,0:T(8,128)(2,1)} fusion(f32[2,17,512,512]{3,2,1,0:T(8,128)} %fusion.253, bf16[2,512,17,64]{1,3,2,0:T(8,128)(2,1)} %bitcast.274, bf16[2,512,17,64]{1,3,2,0:T(8,128)(2,1)} %get-tuple-element.722, f32[2,17,512]{2,1,0:T(8,128)S(1)} %get-tuple-element.723, f32[2,17,512]{2,1,0:T(8,128)S(1)} %get-tuple-element.721, ...), kind=kOutput, calls=%fused_computation.27.clone.1 | convolution fusion | flops 1194328064 | bytes 58597376 | tf_op jit(solution)/shard_map/while/body/eval_jaxpr/sqhd,skhd->shqk/dot_general | solution.py:217
  1348.0 12.2 bitcast_add_fusion.5
  1360.2 9.9 broadcast_multiply_fusion.8
  1378.7 15.5 fusion.253
  1394.2 16.5 fusion.255
  1410.8 22.0 %fusion.254 = bf16[2,17,512,512]{2,3,1,0:T(8,128)(2,1)} fusion(f32[2,17,512,512]{3,2,1,0:T(8,128)} %fusion.253, bf16[2,512,17,64]{1,3,2,0:T(8,128)(2,1)} %bitcast.274, bf16[2,512,17,64]{1,3,2,0:T(8,128)(2,1)} %get-tuple-element.722, f32[2,17,512]{2,1,0:T(8,128)S(1)} %get-tuple-element.723, f32[2,17,512]{2,1,0:T(8,128)S(1)} %get-tuple-element.721, ...), kind=kOutput, calls=%fused_computation.27.clone.1 | convolution fusion | flops 1194328064 | bytes 58597376 | tf_op jit(solution)/shard_map/while/body/eval_jaxpr/sqhd,skhd->shqk/dot_general | solution.py:217
  1432.7 12.2 bitcast_add_fusion.5
  1445.0 9.9 broadcast_multiply_fusion.8
  1462.7 18.8 fusion.71
  1489.6 264.0 %reduce-scatter.34.cloned.1.call-done = bf16[2,512,2176]{1,2,0:T(8,128)(2,1)} async-done(((bf16[2,2048,2176]{1,2,0:T(8,128)(2,1)}), bf16[2,512,2176]{1,2,0:T(8,128)(2,1)}) %reduce-scatter.34.cloned.1.call-update) | async-done | bytes 4456464 | tf_op jit(solution)/shard_map/reduce_scatter | solution.py:248
  1768.4 15.0 fusion.158
  1785.2 20.7 %reduce-scatter.54.cloned.1.call-done = bf16[816,128]{1,0:T(8,128)(2,1)} async-done(((bf16[3264,128]{1,0:T(8,128)(2,1)}), bf16[816,128]{1,0:T(8,128)(2,1)}) %reduce-scatter.54.cloned.1.call-update) | async-done | bytes 208912
  1807.8 6.5 fusion.69
  1814.2 26.2 %reduce-scatter.36.cloned.1.call-done = bf16[16,272]{1,0:T(8,128)(2,1)} async-done(((bf16[128,272]{1,0:T(8,128)(2,1)}), bf16[16,272]{1,0:T(8,128)(2,1)}) %reduce-scatter.36.cloned.1.call-update) | async-done | bytes 8720 | tf_op jit(solution)/shard_map/reduce_scatter | solution.py:307
  1841.7 33.8 %reduce-scatter.38.cloned.1.call-done = bf16[16,816]{1,0:T(8,128)(2,1)} async-done(((bf16[128,816]{1,0:T(8,128)(2,1)}), bf16[16,816]{1,0:T(8,128)(2,1)}) %reduce-scatter.38.cloned.1.call-update) | async-done | bytes 26128 | tf_op jit(solution)/shard_map/reduce_scatter | solution.py:310
  (354 shorter events, 205.4 us)
Async XLA Ops:
  7.2 234.6 %copy-start = (bf16[128,4352]{1,0:T(8,128)(2,1)S(1)}, bf16[128,4352]{1,0:T(8,128)(2,1)}, u32[]{:S(2)}) copy-start(bf16[128,4352]{1,0:T(8,128)(2,1)} %param.36) | copy-start | bytes 3342340
  7.2 33.9 %all-gather.23.cloned.1.call-start = ((), (), s32[]{:S(2)}) async-start(), calls=%async_computation.32 | async-start | bytes 2506752 | tf_op jit(solution)/shard_map/all_gather | solution.py:62
  7.9 44.3 %copy-start.8 = (bf16[2,512,1088]{1,2,0:T(8,128)(2,1)S(1)}, bf16[2,512,1088]{1,2,0:T(8,128)(2,1)}, u32[]{:S(2)}) copy-start(bf16[2,512,1088]{1,2,0:T(8,128)(2,1)} %param.22) | copy-start | bytes 6684676
  7.9 173.6 %all-gather.11.cloned.1.call-start = ((), (), s32[]{:S(2)}) async-start(), calls=%async_computation.17 | async-start | bytes 9052160 | tf_op jit(solution)/shard_map/all_gather | solution.py:68
  50.5 8.0 copy-start.43
  50.5 166.5 %all-gather.25.cloned.1.call-start = ((), (), s32[]{:S(2)}) async-start(), calls=%async_computation.33 | async-start | bytes 3133440 | tf_op jit(solution)/shard_map/all_gather | solution.py:64
  51.3 202.7 %all-gather.19.cloned.1.call-start = ((), (), s32[]{:S(2)}) async-start(), calls=%async_computation.21 | async-start | bytes 2820096 | tf_op jit(solution)/shard_map/all_gather | solution.py:65
  51.8 502.4 %all-gather.13.cloned.1.call-start = ((), (), s32[]{:S(2)}) async-start(), calls=%async_computation.18 | async-start | bytes 22282240 | tf_op jit(solution)/shard_map/all_gather | solution.py:144
  59.8 3.9 copy-start.33
  61.5 132.5 %copy-start.26 = (bf16[2,16,3264]{2,0,1:T(2,128)(2,1)}, bf16[2,16,3264]{2,0,1:T(2,128)(2,1)S(1)}, u32[]{:S(2)}) copy-start(bf16[2,16,3264]{2,0,1:T(2,128)(2,1)S(1)} %convolution_convert_fusion.5) | copy-start | bytes 626692
  65.5 128.6 %copy-start.47 = (bf16[2,512,16]{1,2,0:T(8,128)(2,1)}, bf16[2,512,16]{1,2,0:T(8,128)(2,1)S(1)}, u32[]{:S(2)}) copy-start(bf16[2,512,16]{1,2,0:T(8,128)(2,1)S(1)} %convolution_convert_fusion.21) | copy-start | bytes 98308
  201.1 580.5 %all-gather.15.cloned.1.call-start = ((), (), s32[]{:S(2)}) async-start(), calls=%async_computation.19 | async-start | bytes 3133440 | tf_op jit(solution)/shard_map/all_gather | solution.py:69
  216.3 585.2 %all-gather.17.cloned.1.call-start = ((), (), s32[]{:S(2)}) async-start(), calls=%async_computation.20 | async-start | bytes 11837440 | tf_op jit(solution)/shard_map/all_gather | solution.py:70
  220.9 14.0 copy-start.44
  226.6 18.4 copy-start.19
  226.6 724.9 %all-gather.21.cloned.1.call-start = ((), (), s32[]{:S(2)}) async-start(), calls=%async_computation.22 | async-start | bytes 12533760 | tf_op jit(solution)/shard_map/all_gather | solution.py:71
  244.9 9.0 copy-start.23
  245.3 8.6 copy-start.28
  259.2 295.1 %slice-start = ((bf16[2,512,3264]{1,2,0:T(8,128)(2,1)}), bf16[2,512,1088]{1,2,0:T(8,128)(2,1)S(1)}, s32[]{:S(2)}) async-start(bf16[2,512,3264]{1,2,0:T(8,128)(2,1)} %copy-done.2), calls=%async_computation.42 | async-start | bytes 4456448 | tf_op jit(solution)/shard_map/slice | solution.py:118
  259.2 778.0 %reduce-scatter.66.cloned.1.call-start = ((), (), s32[]{:S(2)}) async-start(), calls=%async_computation.41 | async-start | bytes 348160
  781.5 6.3 copy-start.38
  781.5 6.3 copy-start.9
  789.6 3.3 copy-start.22
  801.5 28.2 %copy-start.24 = (bf16[2,16,4352]{2,0,1:T(2,128)(2,1)S(1)}, bf16[2,16,4352]{2,0,1:T(2,128)(2,1)}, u32[]{:S(2)}) copy-start(bf16[2,16,4352]{2,0,1:T(2,128)(2,1)} %copy-done.23) | copy-start | bytes 835588
  829.7 6.2 copy-start.20
  829.7 6.8 copy-start.45
  835.9 142.4 %copy-start.39 = (bf16[2,512,16]{1,2,0:T(8,128)(2,1)}, bf16[2,512,16]{1,2,0:T(8,128)(2,1)S(1)}, u32[]{:S(2)}) copy-start(bf16[2,512,16]{1,2,0:T(8,128)(2,1)S(1)} %convolution_convert_fusion.17) | copy-start | bytes 98308
  837.9 201.1 %reduce-scatter.60.cloned.1.call-start = ((), (), s32[]{:S(2)}) async-start(), calls=%async_computation.38 | async-start | bytes 348160
  978.3 6.1 copy-start.18
  984.4 4.9 copy-start.55
  989.2 51.5 %reduce-scatter.58.cloned.1.call-start = ((), (), s32[]{:S(2)}) async-start(), calls=%async_computation.37 | async-start | bytes 348160
  989.3 17.1 copy-start.21
  1014.0 5.1 copy-start.29
  1014.0 38.5 %reduce-scatter.56.cloned.1.call-start = ((), (), s32[]{:S(2)}) async-start(), calls=%async_computation.36 | async-start | bytes 348160
  1019.1 62.2 %reduce-scatter.64.cloned.1.call-start = ((), (), s32[]{:S(2)}) async-start(), calls=%async_computation.40 | async-start | bytes 1392640
  1028.1 82.3 %reduce-scatter.62.cloned.1.call-start = ((), (), s32[]{:S(2)}) async-start(), calls=%async_computation.39 | async-start | bytes 1392640
  1037.1 444.3 %reduce-scatter.50.cloned.1.call-start = ((), (), s32[]{:S(2)}) async-start(), calls=%async_computation.31 | async-start | bytes 110592 | tf_op jit(solution)/shard_map/reduce_scatter | solution.py:328
  1038.9 443.9 %reduce-scatter.44.cloned.1.call-start = ((), (), s32[]{:S(2)}) async-start(), calls=%async_computation.28 | async-start | bytes 110592 | tf_op jit(solution)/shard_map/reduce_scatter | solution.py:319
  1040.6 443.5 %reduce-scatter.42.cloned.1.call-start = ((), (), s32[]{:S(2)}) async-start(), calls=%async_computation.27 | async-start | bytes 110592 | tf_op jit(solution)/shard_map/reduce_scatter | solution.py:316
  1042.3 443.1 %reduce-scatter.40.cloned.1.call-start = ((), (), s32[]{:S(2)}) async-start(), calls=%async_computation.26 | async-start | bytes 110592 | tf_op jit(solution)/shard_map/reduce_scatter | solution.py:313
  1054.2 29.0 %copy-start.32 = (bf16[2,16,1088]{2,0,1:T(2,128)(2,1)S(1)}, bf16[2,16,1088]{2,0,1:T(2,128)(2,1)}, u32[]{:S(2)}) copy-start(bf16[2,16,1088]{2,0,1:T(2,128)(2,1)} %convolution_convert_fusion.14) | copy-start | bytes 208900
  1054.2 29.0 %copy-start.42 = (bf16[2,512,16]{1,2,0:T(8,128)(2,1)S(1)}, bf16[2,512,16]{1,2,0:T(8,128)(2,1)}, u32[]{:S(2)}) copy-start(bf16[2,512,16]{1,2,0:T(8,128)(2,1)} %copy-done.41) | copy-start | bytes 98308
  1054.2 432.6 %reduce-scatter.48.cloned.1.call-start = ((), (), s32[]{:S(2)}) async-start(), calls=%async_computation.30 | async-start | bytes 331776 | tf_op jit(solution)/shard_map/reduce_scatter | solution.py:325
  1083.1 405.1 %reduce-scatter.46.cloned.1.call-start = ((), (), s32[]{:S(2)}) async-start(), calls=%async_computation.29 | async-start | bytes 331776 | tf_op jit(solution)/shard_map/reduce_scatter | solution.py:322
  1112.2 641.3 %reduce-scatter.34.cloned.1.call-start = ((), (), s32[]{:S(2)}) async-start(), calls=%async_computation.23 | async-start | bytes 22282240 | tf_op jit(solution)/shard_map/reduce_scatter | solution.py:248
  1190.3 10.0 copy-start.11
  1275.3 10.0 copy-start.11
  1360.2 9.9 copy-start.11
  1445.0 9.9 copy-start.11
  1457.6 325.9 %reduce-scatter.52.cloned.1.call-start = ((), (), s32[]{:S(2)}) async-start(), calls=%async_computation.34 | async-start | bytes 348160
  1458.4 3.6 copy-start.5
  1462.7 297.1 %copy-start.25 = (bf16[2,512,17,64]{1,3,2,0:T(8,128)(2,1)}, bf16[2,512,17,64]{1,3,2,0:T(8,128)(2,1)S(1)}, u32[]{:S(2)}) copy-start(bf16[2,512,17,64]{1,3,2,0:T(8,128)(2,1)S(1)} %multiply_convert_fusion.1) | copy-start | bytes 6684676
  1462.7 290.9 %copy-start.27 = (bf16[2,16,3264]{2,0,1:T(2,128)(2,1)S(1)}, bf16[2,16,3264]{2,0,1:T(2,128)(2,1)}, u32[]{:S(2)}) copy-start(bf16[2,16,3264]{2,0,1:T(2,128)(2,1)} %copy-done.26) | copy-start | bytes 626692
  1753.6 4.2 copy-start.14
  1753.6 4.8 copy-start.46
  1753.6 6.2 copy-start.48
  1759.7 46.2 %reduce-scatter.54.cloned.1.call-start = ((), (), s32[]{:S(2)}) async-start(), calls=%async_computation.35 | async-start | bytes 1044480
  1764.0 4.4 copy-start.10
  1764.0 4.4 copy-start.51
  1764.0 4.4 copy-start.53
  1764.0 4.4 copy-start.56
  1768.3 72.1 %reduce-scatter.36.cloned.1.call-start = ((), (), s32[]{:S(2)}) async-start(), calls=%async_computation.24 | async-start | bytes 110592 | tf_op jit(solution)/shard_map/reduce_scatter | solution.py:307
  1785.1 90.4 %reduce-scatter.38.cloned.1.call-start = ((), (), s32[]{:S(2)}) async-start(), calls=%async_computation.25 | async-start | bytes 258048 | tf_op jit(solution)/shard_map/reduce_scatter | solution.py:310
  1807.8 69.1 %copy-start.1 = (bf16[128,4352]{1,0:T(8,128)(2,1)S(1)}, bf16[128,4352]{1,0:T(8,128)(2,1)}, u32[]{:S(2)}) copy-start(bf16[128,4352]{1,0:T(8,128)(2,1)} %param.36) | copy-start | bytes 3342340
  (28 other events, 47.9 us)
Sparse Core Ops, SparseCore 0:
  9.9 31.1 all-gather.22
  50.7 130.8 all-gather.10
  183.5 31.4 all-gather.24
  216.7 30.4 all-gather.18
  248.7 305.5 all-gather.12
  555.7 51.8 all-gather.14
  609.1 166.0 all-gather.16
  776.8 174.6 all-gather.20
  953.8 18.0 reduce-scatter.65
  989.3 18.0 reduce-scatter.59
  1014.2 18.0 reduce-scatter.57
  1034.4 18.1 reduce-scatter.55
  1054.8 26.3 reduce-scatter.63
  1083.5 26.8 reduce-scatter.61
  1113.2 31.0 reduce-scatter.49
  1147.2 32.4 reduce-scatter.43
  1182.6 32.4 reduce-scatter.41
  1217.9 32.4 reduce-scatter.39
  1253.5 32.8 reduce-scatter.47
  1289.3 32.9 reduce-scatter.45
  1457.7 295.8 reduce-scatter.33
  1759.8 20.7 reduce-scatter.51
  1783.6 22.2 reduce-scatter.53
  1808.8 31.5 reduce-scatter.35
  1843.5 31.9 reduce-scatter.37
where the time goes:
time: 1890 us; the launch traced here: 1880 us
  waiting for transfers between devices  951 us (50%)
  matrix products  663 us (35%)
  local copies, waits for them, and re-layouts  129 us (7%)
  other arithmetic  109 us (6%)
    all_gather x1, waiting for transfers between devices, per_device(): piece = lax.all_gather(key_vals, 'ctx', axis=1, tiled=True)  295 us
    reduce_scatter x1, waiting for transfers between devices, per_device(): lax.psum_scatter(grad_keys.astype(jnp.bfloat16), 'ctx', scatter_dimension...  264 us
    all_gather x1, waiting for transfers between devices, gather_weights(): lax.all_gather(wide_qkv, 'ctx', axis=0, tiled=True)  116 us
    all_gather x1, waiting for transfers between devices, gather_weights(): lax.all_gather(wide_fc2, 'ctx', axis=0, tiled=True)  114 us
    dot_general x4, matrix products, back_step(): jnp.einsum('sqhd,skhd->shqk', grad_att_heads, values, preferred_element_t...  88 us
    dot_general x4, matrix products, attend(): jnp.einsum('shqk,skhd->sqhd', expo_term.astype(jnp.bfloat16), values, pre...  77.4 us
    unnamed x33, waiting for transfers between devices  69.1 us
    dot_general x4, matrix products, project_back(): jnp.einsum('slv,wv->slw', grad_low, weight, preferred_element_type=jnp.fl...  67.1 us
  transfers between devices with their start and end apart: 25, of which 11 were waited for; matrix products, arithmetic and copies ran while one was open for 46% of the time, Pallas kernels for 0%

commit v1 on v0

--- a/solution.py
+++ b/solution.py
@@ -7,6 +7,17 @@
 ADAPTERS = 8
 eps = 1e-05
 neg_big = -1e30
+
+
+def ring_gather(x, axis, dim):
+    ways = lax.axis_size(axis)
+    pieces = [x]
+    for far in range(1, ways):
+        pieces.append(
+            lax.ppermute(pieces[far - 1], axis, [(d, (d - 1) % ways) for d in range(ways)])
+        )
+    line = jnp.concatenate(pieces, axis=dim)
+    return jnp.roll(line, lax.axis_index(axis) * x.shape[dim], axis=dim)
 
 
 def norm_rows(vector, gain):
@@ -68,7 +79,7 @@
         lax.all_gather(wide_qkv, "ctx", axis=0, tiled=True),
         lax.all_gather(wide_out, "ctx", axis=0, tiled=True),
         lax.all_gather(wide_fc1, "ctx", axis=0, tiled=True),
-        lax.all_gather(wide_fc2, "ctx", axis=0, tiled=True),
+        ring_gather(wide_fc2, "ctx", 0),
     )
 
 

time: 1890 us -> 1890 us (level)
    ppermute x0 -> x3, waiting for transfers between devices: none -> 349 us  [ring_gather(): lax.ppermute(pieces[far - 1], axis, [(d, (d - 1) % ways) for d in range(w...]
    all_gather x1, waiting for transfers between devices: 295 us -> 28.2 us  [per_device(): piece = lax.all_gather(key_vals, 'ctx', axis=1, tiled=True)]
    all_gather x1 -> x0, waiting for transfers between devices: 114 us -> none  [gather_weights(): lax.all_gather(wide_fc2, 'ctx', axis=0, tiled=True)]
    unnamed x33 -> x32, waiting for transfers between devices: 69.1 us -> 76.7 us
    unnamed x132 -> x134, local copies, waits for them, and re-layouts: 61.5 us -> 56.9 us
  transfers between devices with their start and end apart: 25 -> 27, of which waited for: 11 -> 14; matrix products, arithmetic and copies ran while one was open for 46% -> 45% of each run, Pallas kernels for 0% -> 0%
where the time goes in v1:
time: 1890 us; the launch traced here: 1880 us
  waiting for transfers between devices  936 us (50%)
  matrix products  663 us (35%)
  local copies, waits for them, and re-layouts  133 us (7%)
  other arithmetic  110 us (6%)
    ppermute x3, waiting for transfers between devices, ring_gather(): lax.ppermute(pieces[far - 1], axis, [(d, (d - 1) % ways) for d in range(w...  349 us
    reduce_scatter x1, waiting for transfers between devices, per_device(): lax.psum_scatter(grad_keys.astype(jnp.bfloat16), 'ctx', scatter_dimension...  263 us
    all_gather x1, waiting for transfers between devices, gather_weights(): lax.all_gather(wide_qkv, 'ctx', axis=0, tiled=True)  116 us
    dot_general x4, matrix products, back_step(): jnp.einsum('sqhd,skhd->shqk', grad_att_heads, values, preferred_element_t...  88.1 us
    dot_general x4, matrix products, attend(): jnp.einsum('shqk,skhd->sqhd', expo_term.astype(jnp.bfloat16), values, pre...  77.4 us
    unnamed x32, waiting for transfers between devices  76.7 us
    dot_general x4, matrix products, project_back(): jnp.einsum('slv,wv->slw', grad_low, weight, preferred_element_type=jnp.fl...  74.9 us
    dot_general x4, matrix products, back_step(): jnp.einsum('shqk,sqhd->skhd', probs.astype(jnp.bfloat16), grad_att_heads,...  66.6 us
  transfers between devices with their start and end apart: 27, of which 14 were waited for; matrix products, arithmetic and copies ran while one was open for 45% of the time, Pallas kernels for 0%

profile of v1, /device:TPU:0, one launch (start us, length us, event | category | flops | bytes accessed | tf_op | source)
XLA Modules:
  0.0 1879.1 jit_solution(18049242421606448883)
XLA Ops:
  8.0 33.1 %all-gather.20.cloned.1.call-done = bf16[8,408,272]{1,2,0:T(8,128)(2,1)} async-done(((bf16[1,408,272]{1,2,0:T(8,128)(2,1)}), bf16[8,408,272]{1,2,0:T(8,128)(2,1)}) %all-gather.20.cloned.1.call-update) | async-done | bytes 1775632 | tf_op jit(solution)/shard_map/all_gather | solution.py:73
  65.7 115.9 %all-gather.10.cloned.1.call-done = bf16[1088,3264]{1,0:T(8,128)(2,1)} async-done(((bf16[272,3264]{1,0:T(8,128)(2,1)}), bf16[1088,3264]{1,0:T(8,128)(2,1)}) %all-gather.10.cloned.1.call-update) | async-done | bytes 7102480 | tf_op jit(solution)/shard_map/all_gather | solution.py:79
  181.6 12.5 fusion.38
  201.1 10.2 all-gather.18.cloned.1.call-done
  214.7 63.7 %collective-permute-done = bf16[1088,1088]{0,1:T(8,128)(2,1)} collective-permute-done((bf16[1088,1088]{0,1:T(8,128)(2,1)}, bf16[1088,1088]{0,1:T(8,128)(2,1)}, u32[]{:S(2)}, u32[]{:S(2)}) %collective-permute-start) | collective-permute-done | bytes 2367520 | tf_op jit(solution)/shard_map/ppermute | solution.py:17
  282.7 11.2 all_gather.35
  304.5 147.5 %collective-permute-done.1 = bf16[1088,1088]{0,1:T(8,128)(2,1)} collective-permute-done((bf16[1088,1088]{0,1:T(8,128)(2,1)}, bf16[1088,1088]{0,1:T(8,128)(2,1)}, u32[]{:S(2)}, u32[]{:S(2)}) %collective-permute-start.1) | collective-permute-done | bytes 2367520 | tf_op jit(solution)/shard_map/ppermute | solution.py:17
  462.6 8.6 fusion.87
  480.9 138.2 %collective-permute-done.2 = bf16[1088,1088]{0,1:T(8,128)(2,1)} collective-permute-done((bf16[1088,1088]{0,1:T(8,128)(2,1)}, bf16[1088,1088]{0,1:T(8,128)(2,1)}, u32[]{:S(2)}, u32[]{:S(2)}) %collective-permute-start.2) | collective-permute-done | bytes 2367520 | tf_op jit(solution)/shard_map/ppermute | solution.py:17
  619.1 16.1 concatenate.18
  635.2 28.2 %all-gather.12.cloned.1.call-done = bf16[2,2048,2176]{1,2,0:T(8,128)(2,1)} async-done(((bf16[2,512,2176]{1,2,0:T(8,128)(2,1)}), bf16[2,2048,2176]{1,2,0:T(8,128)(2,1)}) %all-gather.12.cloned.1.call-update) | async-done | bytes 17825808 | tf_op jit(solution)/shard_map/all_gather | solution.py:155
  663.4 221.2 %while.34 = (s32[]{:T(128)}, f32[2,17,512]{2,1,0:T(8,128)S(1)}, f32[2,17,512]{2,1,0:T(8,128)S(1)}, f32[2,512,17,64]{1,3,2,0:T(8,128)}, s32[2,2048]{1,0:T(2,128)}...) while((s32[]{:T(128)}, f32[2,17,512]{2,1,0:T(8,128)S(1)}, ...), condition=%wide.region_5.6_spmd.clone, body=%wide.region_2.5_spmd.clone.sunk | while | flops 2402327552 | bytes 135225584 | solution.py:169
  668.8 14.8 fusion.237
  683.6 15.4 fusion.239
  699.0 17.9 bitcast_add_fusion.5
  722.4 16.3 fusion.237
  738.7 15.4 fusion.239
  754.1 20.0 %bitcast_add_fusion.5 = f32[2,512,17,64]{1,3,2,0:T(8,128)} fusion(f32[2,512,17,64]{1,3,2,0:T(8,128)} %get-tuple-element.658, f32[2,512,17]{1,2,0:T(8,128)S(1)} %get-tuple-element.624, pred[]{:T(512)S(6)} %compare.6, bf16[2,512,17,64]{1,3,2,0:T(8,128)(2,1)} %bitcast.268, f32[2,17,512,512]{3,2,1,0:T(8,128)} %get-tuple-element.623, ...), kind=kOutput, calls=%fused_computation.9.clone.1 | convolution fusion | flops 1188757504 | bytes 47456256 | tf_op jit(solution)/shard_map/while/body/eval_jaxpr/shqk,skhd->sqhd/dot_general | solution.py:142
  779.6 14.5 fusion.237
  794.2 15.4 fusion.239
  809.5 20.0 %bitcast_add_fusion.5 = f32[2,512,17,64]{1,3,2,0:T(8,128)} fusion(f32[2,512,17,64]{1,3,2,0:T(8,128)} %get-tuple-element.658, f32[2,512,17]{1,2,0:T(8,128)S(1)} %get-tuple-element.624, pred[]{:T(512)S(6)} %compare.6, bf16[2,512,17,64]{1,3,2,0:T(8,128)(2,1)} %bitcast.268, f32[2,17,512,512]{3,2,1,0:T(8,128)} %get-tuple-element.623, ...), kind=kOutput, calls=%fused_computation.9.clone.1 | convolution fusion | flops 1188757504 | bytes 47456256 | tf_op jit(solution)/shard_map/while/body/eval_jaxpr/shqk,skhd->sqhd/dot_general | solution.py:142
  835.0 14.3 fusion.237
  849.3 15.3 fusion.239
  864.6 19.5 %bitcast_add_fusion.5 = f32[2,512,17,64]{1,3,2,0:T(8,128)} fusion(f32[2,512,17,64]{1,3,2,0:T(8,128)} %get-tuple-element.658, f32[2,512,17]{1,2,0:T(8,128)S(1)} %get-tuple-element.624, pred[]{:T(512)S(6)} %compare.6, bf16[2,512,17,64]{1,3,2,0:T(8,128)(2,1)} %bitcast.268, f32[2,17,512,512]{3,2,1,0:T(8,128)} %get-tuple-element.623, ...), kind=kOutput, calls=%fused_computation.9.clone.1 | convolution fusion | flops 1188757504 | bytes 47456256 | tf_op jit(solution)/shard_map/while/body/eval_jaxpr/shqk,skhd->sqhd/dot_general | solution.py:142
  901.8 8.7 fusion.91
  910.5 25.4 %multiply_convert_fusion = (bf16[2,512,4352]{2,1,0:T(8,128)(2,1)}, f32[2,512,4352]{2,1,0:T(8,128)}) fusion(f32[2,512,4352]{2,1,0:T(8,128)} %fusion.91, bf16[2,512,1088]{1,2,0:T(8,128)(2,1)S(1)} %multiply_convert_fusion.2, bf16[1088,4352]{1,0:T(8,128)(2,1)} %all-gather.16.cloned.1.call-done), kind=kOutput, calls=%fused_computation.56 | convolution fusion | flops 9741795328 | bytes 56262656 | tf_op jit(solution)/shard_map/slw,wv->slv/dot_general | solution.py:47
  935.9 6.1 convolution_convert_fusion.17
  944.0 34.3 %fusion.30 = bf16[2,512,4352]{2,1,0:T(8,128)(2,1)} fusion(f32[2,512,4352]{2,1,0:T(8,128)} %get-tuple-element.488, f32[2,512,4352]{2,1,0:T(8,128)} %fusion.87, bf16[2,512,1088]{1,2,0:T(8,128)(2,1)} %param.41, s32[]{:T(128)S(6)} %select_n.59, bf16[4352,1088]{0,1:T(8,128)(2,1)} %concatenate.18), kind=kOutput, calls=%fused_computation.54 | convolution fusion | flops 9809756160 | bytes 56262660 | tf_op jit(solution)/shard_map/slv,wv->slw/dot_general | solution.py:59
  978.4 5.9 convolution_convert_fusion.16
  989.2 17.3 fusion.157
  1038.3 17.2 reduce-scatter.56.cloned.1.call-done
  1057.3 8.1 fusion.67
  1065.4 19.3 %reduce-scatter.64.cloned.1.call-done = bf16[1088,128]{1,0:T(8,128)(2,1)} async-done(((bf16[4352,128]{1,0:T(8,128)(2,1)}), bf16[1088,128]{1,0:T(8,128)(2,1)}) %reduce-scatter.64.cloned.1.call-update) | async-done | bytes 278544
  1086.6 7.2 bitcast_multiply_fusion.1
  1096.8 17.2 reduce-scatter.62.cloned.1.call-done
  1115.9 6.4 broadcast_in_dim.126
  1122.4 330.3 %while.35 = (s32[]{:T(128)}, f32[2,512,17,64]{1,3,2,0:T(8,128)}, bf16[2,2048,2176]{1,2,0:T(8,128)(2,1)}, bf16[2,2048,2176]{1,2,0:T(8,128)(2,1)}, s32[2,2048]{1,0...) while((s32[]{:T(128)}, f32[2,512,17,64]{1,3,2,0:T(8,128)}, ...), condition=%wide.region_12.14_spmd.clone, body=%wide.region_11.13_spmd.clone.sunk | while | flops 5808063488 | bytes 236294480 | solution.py:258
  1128.3 14.0 fusion.251
  1142.3 16.6 fusion.253
  1158.9 22.1 %fusion.252 = bf16[2,17,512,512]{2,3,1,0:T(8,128)(2,1)} fusion(f32[2,17,512,512]{3,2,1,0:T(8,128)} %fusion.251, bf16[2,512,17,64]{1,3,2,0:T(8,128)(2,1)} %bitcast.270, bf16[2,512,17,64]{1,3,2,0:T(8,128)(2,1)} %get-tuple-element.723, f32[2,17,512]{2,1,0:T(8,128)S(1)} %get-tuple-element.724, f32[2,17,512]{2,1,0:T(8,128)S(1)} %get-tuple-element.722, ...), kind=kOutput, calls=%fused_computation.27.clone.1 | convolution fusion | flops 1194328064 | bytes 58597376 | tf_op jit(solution)/shard_map/while/body/eval_jaxpr/sqhd,skhd->shqk/dot_general | solution.py:228
  1180.9 11.1 bitcast_add_fusion.6
  1192.1 9.6 broadcast_multiply_fusion.8
  1209.7 14.0 fusion.251
  1223.7 16.7 fusion.253
  1240.4 22.0 %fusion.252 = bf16[2,17,512,512]{2,3,1,0:T(8,128)(2,1)} fusion(f32[2,17,512,512]{3,2,1,0:T(8,128)} %fusion.251, bf16[2,512,17,64]{1,3,2,0:T(8,128)(2,1)} %bitcast.270, bf16[2,512,17,64]{1,3,2,0:T(8,128)(2,1)} %get-tuple-element.723, f32[2,17,512]{2,1,0:T(8,128)S(1)} %get-tuple-element.724, f32[2,17,512]{2,1,0:T(8,128)S(1)} %get-tuple-element.722, ...), kind=kOutput, calls=%fused_computation.27.clone.1 | convolution fusion | flops 1194328064 | bytes 58597376 | tf_op jit(solution)/shard_map/while/body/eval_jaxpr/sqhd,skhd->shqk/dot_general | solution.py:228
  1262.5 12.6 bitcast_add_fusion.6
  1275.0 9.6 broadcast_multiply_fusion.8
  1292.8 14.2 fusion.251
  1306.9 16.7 fusion.253
  1323.6 22.0 %fusion.252 = bf16[2,17,512,512]{2,3,1,0:T(8,128)(2,1)} fusion(f32[2,17,512,512]{3,2,1,0:T(8,128)} %fusion.251, bf16[2,512,17,64]{1,3,2,0:T(8,128)(2,1)} %bitcast.270, bf16[2,512,17,64]{1,3,2,0:T(8,128)(2,1)} %get-tuple-element.723, f32[2,17,512]{2,1,0:T(8,128)S(1)} %get-tuple-element.724, f32[2,17,512]{2,1,0:T(8,128)S(1)} %get-tuple-element.722, ...), kind=kOutput, calls=%fused_computation.27.clone.1 | convolution fusion | flops 1194328064 | bytes 58597376 | tf_op jit(solution)/shard_map/while/body/eval_jaxpr/sqhd,skhd->shqk/dot_general | solution.py:228
  1345.6 12.4 bitcast_add_fusion.6
  1358.0 9.5 broadcast_multiply_fusion.8
  1375.6 14.0 fusion.251
  1389.5 16.6 fusion.253
  1406.1 22.0 %fusion.252 = bf16[2,17,512,512]{2,3,1,0:T(8,128)(2,1)} fusion(f32[2,17,512,512]{3,2,1,0:T(8,128)} %fusion.251, bf16[2,512,17,64]{1,3,2,0:T(8,128)(2,1)} %bitcast.270, bf16[2,512,17,64]{1,3,2,0:T(8,128)(2,1)} %get-tuple-element.723, f32[2,17,512]{2,1,0:T(8,128)S(1)} %get-tuple-element.724, f32[2,17,512]{2,1,0:T(8,128)S(1)} %get-tuple-element.722, ...), kind=kOutput, calls=%fused_computation.27.clone.1 | convolution fusion | flops 1194328064 | bytes 58597376 | tf_op jit(solution)/shard_map/while/body/eval_jaxpr/sqhd,skhd->shqk/dot_general | solution.py:228
  1428.1 12.4 bitcast_add_fusion.6
  1440.5 9.5 broadcast_multiply_fusion.8
  1457.8 20.0 %fusion.65 = bf16[2,512,1088]{1,2,0:T(8,128)(2,1)} fusion(f32[2,512,1088]{1,2,0:T(8,128)} %copy-done.8, f32[2,512,1088]{1,2,0:T(8,128)} %fusion.101, bf16[2,512,4352]{2,1,0:T(8,128)(2,1)} %get-tuple-element.487, s32[]{:T(128)S(6)} %select_n.59, bf16[4352,1088]{0,1:T(8,128)(2,1)} %concatenate.18), kind=kOutput, calls=%fused_computation.106 | convolution fusion | flops 9719513088 | bytes 29523972 | tf_op jit(solution)/shard_map/slw,wv->slv/dot_general | solution.py:47
  1485.9 262.7 %reduce-scatter.34.cloned.1.call-done = bf16[2,512,2176]{1,2,0:T(8,128)(2,1)} async-done(((bf16[2,2048,2176]{1,2,0:T(8,128)(2,1)}), bf16[2,512,2176]{1,2,0:T(8,128)(2,1)}) %reduce-scatter.34.cloned.1.call-update) | async-done | bytes 4456464 | tf_op jit(solution)/shard_map/reduce_scatter | solution.py:259
  1763.5 15.1 fusion.156
  1780.3 20.7 %reduce-scatter.54.cloned.1.call-done = bf16[816,128]{1,0:T(8,128)(2,1)} async-done(((bf16[3264,128]{1,0:T(8,128)(2,1)}), bf16[816,128]{1,0:T(8,128)(2,1)}) %reduce-scatter.54.cloned.1.call-update) | async-done | bytes 208912
  1802.8 6.5 fusion.63
  1809.3 26.4 %reduce-scatter.36.cloned.1.call-done = bf16[16,272]{1,0:T(8,128)(2,1)} async-done(((bf16[128,272]{1,0:T(8,128)(2,1)}), bf16[16,272]{1,0:T(8,128)(2,1)}) %reduce-scatter.36.cloned.1.call-update) | async-done | bytes 8720 | tf_op jit(solution)/shard_map/reduce_scatter | solution.py:318
  1837.0 33.6 %reduce-scatter.38.cloned.1.call-done = bf16[16,816]{1,0:T(8,128)(2,1)} async-done(((bf16[128,816]{1,0:T(8,128)(2,1)}), bf16[16,816]{1,0:T(8,128)(2,1)}) %reduce-scatter.38.cloned.1.call-update) | async-done | bytes 26128 | tf_op jit(solution)/shard_map/reduce_scatter | solution.py:321
  (359 shorter events, 222.9 us)
Async XLA Ops:
  7.2 451.9 %copy-start = (bf16[128,4352]{1,0:T(8,128)(2,1)S(1)}, bf16[128,4352]{1,0:T(8,128)(2,1)}, u32[]{:S(2)}) copy-start(bf16[128,4352]{1,0:T(8,128)(2,1)} %param.38) | copy-start | bytes 3342340
  7.2 33.9 %all-gather.20.cloned.1.call-start = ((), (), s32[]{:S(2)}) async-start(), calls=%async_computation.31 | async-start | bytes 2506752 | tf_op jit(solution)/shard_map/all_gather | solution.py:73
  7.9 44.5 %copy-start.9 = (bf16[2,512,1088]{1,2,0:T(8,128)(2,1)S(1)}, bf16[2,512,1088]{1,2,0:T(8,128)(2,1)}, u32[]{:S(2)}) copy-start(bf16[2,512,1088]{1,2,0:T(8,128)(2,1)} %param.24) | copy-start | bytes 6684676
  7.9 173.6 %all-gather.10.cloned.1.call-start = ((), (), s32[]{:S(2)}) async-start(), calls=%async_computation.17 | async-start | bytes 9052160 | tf_op jit(solution)/shard_map/all_gather | solution.py:79
  50.5 8.2 copy-start.45
  50.5 160.8 %all-gather.18.cloned.1.call-start = ((), (), s32[]{:S(2)}) async-start(), calls=%async_computation.21 | async-start | bytes 2820096 | tf_op jit(solution)/shard_map/all_gather | solution.py:76
  51.3 420.0 %all-gather.22.cloned.1.call-start = ((), (), s32[]{:S(2)}) async-start(), calls=%async_computation.32 | async-start | bytes 3133440 | tf_op jit(solution)/shard_map/all_gather | solution.py:75
  51.8 611.6 %all-gather.12.cloned.1.call-start = ((), (), s32[]{:S(2)}) async-start(), calls=%async_computation.18 | async-start | bytes 22282240 | tf_op jit(solution)/shard_map/all_gather | solution.py:155
  61.7 132.3 %copy-start.29 = (bf16[2,16,3264]{2,0,1:T(2,128)(2,1)}, bf16[2,16,3264]{2,0,1:T(2,128)(2,1)S(1)}, u32[]{:S(2)}) copy-start(bf16[2,16,3264]{2,0,1:T(2,128)(2,1)S(1)} %convolution_convert_fusion.5) | copy-start | bytes 626692
  65.7 128.4 %copy-start.49 = (bf16[2,512,16]{1,2,0:T(8,128)(2,1)}, bf16[2,512,16]{1,2,0:T(8,128)(2,1)S(1)}, u32[]{:S(2)}) copy-start(bf16[2,512,16]{1,2,0:T(8,128)(2,1)S(1)} %convolution_convert_fusion.21) | copy-start | bytes 98308
  201.1 81.6 %copy-start.51 = (bf16[272,136]{0,1:T(8,128)(2,1)S(1)}, bf16[272,136]{0,1:T(8,128)(2,1)}, u32[]{:S(2)}) copy-start(bf16[272,136]{0,1:T(8,128)(2,1)} %param.28) | copy-start | bytes 221956
  201.1 251.1 %copy-start.46 = (s32[2]{0:T(128)S(1)}, s32[2]{0:T(128)}, u32[]{:S(2)}) copy-start(s32[2]{0:T(128)} %param.26) | copy-start | bytes 28
  201.1 691.7 %all-gather.14.cloned.1.call-start = ((), (), s32[]{:S(2)}) async-start(), calls=%async_computation.19 | async-start | bytes 3133440 | tf_op jit(solution)/shard_map/all_gather | solution.py:80
  211.4 67.0 %collective-permute-start = (bf16[1088,1088]{0,1:T(8,128)(2,1)}, bf16[1088,1088]{0,1:T(8,128)(2,1)}, u32[]{:S(2)}, u32[]{:S(2)}) collective-permute-start(bf16[1088,1088]{0,1:T(8,128)(2,1)} %all-gather.18.cloned.1.call-done), channel_id=1, source_target_pairs={{0,3},{1,0},{2,1},{3,2},{4,7},{5,4},{6,5},{7,6},{8,11},{9,8},{10,9... | collective-permute-start | bytes 7102472 | tf_op jit(solution)/shard_map/ppermute | solution.py:17
  278.4 173.6 %collective-permute-start.1 = (bf16[1088,1088]{0,1:T(8,128)(2,1)}, bf16[1088,1088]{0,1:T(8,128)(2,1)}, u32[]{:S(2)}, u32[]{:S(2)}) collective-permute-start(bf16[1088,1088]{0,1:T(8,128)(2,1)} %collective-permute-done), channel_id=1, source_target_pairs={{0,3},{1,0},{2,1},{3,2},{4,7},{5,4},{6,5},{7,6},{8,11},{9,8},{10,9... | collective-permute-start | bytes 7102472 | tf_op jit(solution)/shard_map/ppermute | solution.py:17
  293.9 168.3 %copy-start.18 = (bf16[2,512,1088]{1,2,0:T(8,128)(2,1)S(1)}, bf16[2,512,1088]{1,2,0:T(8,128)(2,1)}, u32[]{:S(2)}) copy-start(bf16[2,512,1088]{1,2,0:T(8,128)(2,1)} %param.41) | copy-start | bytes 6684676
  296.4 614.1 %all-gather.16.cloned.1.call-start = ((), (), s32[]{:S(2)}) async-start(), calls=%async_computation.20 | async-start | bytes 11837440 | tf_op jit(solution)/shard_map/all_gather | solution.py:81
  452.0 167.1 %collective-permute-start.2 = (bf16[1088,1088]{0,1:T(8,128)(2,1)}, bf16[1088,1088]{0,1:T(8,128)(2,1)}, u32[]{:S(2)}, u32[]{:S(2)}) collective-permute-start(bf16[1088,1088]{0,1:T(8,128)(2,1)} %collective-permute-done.1), channel_id=1, source_target_pairs={{0,3},{1,0},{2,1},{3,2},{4,7},{5,4},{6,5},{7,6},{8,11},{9,8},{10,9... | collective-permute-start | bytes 7102472 | tf_op jit(solution)/shard_map/ppermute | solution.py:17
  462.2 9.0 copy-start.26
  462.6 8.6 copy-start.31
  480.8 552.3 %reduce-scatter.66.cloned.1.call-start = ((), (), s32[]{:S(2)}) async-start(), calls=%async_computation.40 | async-start | bytes 348160
  635.2 28.2 %slice-start = ((bf16[2,512,3264]{1,2,0:T(8,128)(2,1)}), bf16[2,512,1088]{1,2,0:T(8,128)(2,1)S(1)}, s32[]{:S(2)}) async-start(bf16[2,512,3264]{1,2,0:T(8,128)(2,1)} %copy-done.2), calls=%async_computation.41 | async-start | bytes 4456448 | tf_op jit(solution)/shard_map/slice | solution.py:129
  884.6 13.7 copy-start.3
  892.7 5.7 copy-start.40
  892.7 5.7 copy-start.10
  910.5 25.4 %copy-start.27 = (bf16[2,16,4352]{2,0,1:T(2,128)(2,1)S(1)}, bf16[2,16,4352]{2,0,1:T(2,128)(2,1)}, u32[]{:S(2)}) copy-start(bf16[2,16,4352]{2,0,1:T(2,128)(2,1)} %copy-done.26) | copy-start | bytes 835588
  935.9 6.1 copy-start.19
  935.9 6.8 copy-start.47
  942.0 36.4 %copy-start.43 = (bf16[2,512,16]{1,2,0:T(8,128)(2,1)}, bf16[2,512,16]{1,2,0:T(8,128)(2,1)S(1)}, u32[]{:S(2)}) copy-start(bf16[2,512,16]{1,2,0:T(8,128)(2,1)S(1)} %convolution_convert_fusion.17) | copy-start | bytes 98308
  944.0 90.9 %reduce-scatter.60.cloned.1.call-start = ((), (), s32[]{:S(2)}) async-start(), calls=%async_computation.37 | async-start | bytes 348160
  989.1 17.4 copy-start.20
  989.1 47.5 %reduce-scatter.58.cloned.1.call-start = ((), (), s32[]{:S(2)}) async-start(), calls=%async_computation.36 | async-start | bytes 348160
  1012.2 4.7 copy-start.17
  1014.1 4.8 copy-start.32
  1014.2 41.4 %reduce-scatter.56.cloned.1.call-start = ((), (), s32[]{:S(2)}) async-start(), calls=%async_computation.35 | async-start | bytes 348160
  1018.9 65.8 %reduce-scatter.64.cloned.1.call-start = ((), (), s32[]{:S(2)}) async-start(), calls=%async_computation.39 | async-start | bytes 1392640
  1026.0 88.0 %reduce-scatter.62.cloned.1.call-start = ((), (), s32[]{:S(2)}) async-start(), calls=%async_computation.38 | async-start | bytes 1392640
  1033.1 444.7 %reduce-scatter.50.cloned.1.call-start = ((), (), s32[]{:S(2)}) async-start(), calls=%async_computation.30 | async-start | bytes 110592 | tf_op jit(solution)/shard_map/reduce_scatter | solution.py:339
  1034.8 444.3 %reduce-scatter.44.cloned.1.call-start = ((), (), s32[]{:S(2)}) async-start(), calls=%async_computation.27 | async-start | bytes 110592 | tf_op jit(solution)/shard_map/reduce_scatter | solution.py:330
  1036.6 443.9 %reduce-scatter.42.cloned.1.call-start = ((), (), s32[]{:S(2)}) async-start(), calls=%async_computation.26 | async-start | bytes 110592 | tf_op jit(solution)/shard_map/reduce_scatter | solution.py:327
  1038.3 443.5 %reduce-scatter.40.cloned.1.call-start = ((), (), s32[]{:S(2)}) async-start(), calls=%async_computation.25 | async-start | bytes 110592 | tf_op jit(solution)/shard_map/reduce_scatter | solution.py:324
  1057.2 29.4 %copy-start.34 = (bf16[2,16,1088]{2,0,1:T(2,128)(2,1)S(1)}, bf16[2,16,1088]{2,0,1:T(2,128)(2,1)}, u32[]{:S(2)}) copy-start(bf16[2,16,1088]{2,0,1:T(2,128)(2,1)} %convolution_convert_fusion.14) | copy-start | bytes 208900
  1057.2 425.9 %reduce-scatter.48.cloned.1.call-start = ((), (), s32[]{:S(2)}) async-start(), calls=%async_computation.29 | async-start | bytes 331776 | tf_op jit(solution)/shard_map/reduce_scatter | solution.py:336
  1086.6 398.0 %reduce-scatter.46.cloned.1.call-start = ((), (), s32[]{:S(2)}) async-start(), calls=%async_computation.28 | async-start | bytes 331776 | tf_op jit(solution)/shard_map/reduce_scatter | solution.py:333
  1115.9 632.7 %reduce-scatter.34.cloned.1.call-start = ((), (), s32[]{:S(2)}) async-start(), calls=%async_computation.22 | async-start | bytes 22282240 | tf_op jit(solution)/shard_map/reduce_scatter | solution.py:259
  1115.9 6.4 copy-start.42
  1180.9 11.1 copy-start.5
  1192.1 9.6 copy-start.12
  1262.5 12.6 copy-start.5
  1275.0 9.6 copy-start.12
  1345.6 12.4 copy-start.5
  1358.0 9.5 copy-start.12
  1428.1 12.4 copy-start.5
  1440.5 9.5 copy-start.12
  1452.7 325.9 %reduce-scatter.52.cloned.1.call-start = ((), (), s32[]{:S(2)}) async-start(), calls=%async_computation.33 | async-start | bytes 348160
  1457.8 297.0 %copy-start.28 = (bf16[2,512,17,64]{1,3,2,0:T(8,128)(2,1)}, bf16[2,512,17,64]{1,3,2,0:T(8,128)(2,1)S(1)}, u32[]{:S(2)}) copy-start(bf16[2,512,17,64]{1,3,2,0:T(8,128)(2,1)S(1)} %multiply_convert_fusion.1) | copy-start | bytes 6684676
  1457.8 290.8 %copy-start.30 = (bf16[2,16,3264]{2,0,1:T(2,128)(2,1)S(1)}, bf16[2,16,3264]{2,0,1:T(2,128)(2,1)}, u32[]{:S(2)}) copy-start(bf16[2,16,3264]{2,0,1:T(2,128)(2,1)} %copy-done.29) | copy-start | bytes 626692
  1748.6 4.9 copy-start.48
  1748.6 6.2 copy-start.50
  1754.8 46.2 %reduce-scatter.54.cloned.1.call-start = ((), (), s32[]{:S(2)}) async-start(), calls=%async_computation.34 | async-start | bytes 1044480
  1759.0 4.4 copy-start.11
  1763.4 72.2 %reduce-scatter.36.cloned.1.call-start = ((), (), s32[]{:S(2)}) async-start(), calls=%async_computation.23 | async-start | bytes 110592 | tf_op jit(solution)/shard_map/reduce_scatter | solution.py:318
  1780.2 90.4 %reduce-scatter.38.cloned.1.call-start = ((), (), s32[]{:S(2)}) async-start(), calls=%async_computation.24 | async-start | bytes 258048 | tf_op jit(solution)/shard_map/reduce_scatter | solution.py:321
  1802.8 69.2 %copy-start.1 = (bf16[128,4352]{1,0:T(8,128)(2,1)S(1)}, bf16[128,4352]{1,0:T(8,128)(2,1)}, u32[]{:S(2)}) copy-start(bf16[128,4352]{1,0:T(8,128)(2,1)} %param.38) | copy-start | bytes 3342340
  (31 other events, 86.4 us)
Sparse Core Ops, SparseCore 0:
  9.9 31.1 all-gather.19
  50.7 130.8 all-gather.9
  183.5 27.8 all-gather.17
  213.1 30.7 all-gather.21
  245.4 417.9 all-gather.11
  664.8 53.9 all-gather.13
  720.4 166.0 all-gather.15
  944.1 20.7 reduce-scatter.65
  989.3 20.7 reduce-scatter.59
  1014.3 20.7 reduce-scatter.57
  1037.4 18.1 reduce-scatter.55
  1058.3 26.3 reduce-scatter.63
  1087.1 26.8 reduce-scatter.61
  1116.9 31.0 reduce-scatter.49
  1150.8 32.3 reduce-scatter.43
  1186.1 32.3 reduce-scatter.41
  1221.4 32.3 reduce-scatter.39
  1256.7 32.8 reduce-scatter.47
  1292.7 32.8 reduce-scatter.45
  1452.8 295.7 reduce-scatter.33
  1754.9 20.7 reduce-scatter.51
  1778.6 22.3 reduce-scatter.53
  1804.0 31.5 reduce-scatter.35
  1838.6 31.9 reduce-scatter.37
